TPU v7x, 32 devices: a whole 2x2x4 slice. The times are simulated.
32 devices in a mesh: ia: 2 (over x), ja: 4 (over y, core), ka: 4 (over z).
Axes of the slice: x: 2, y: 2, z: 4, core: 2. Of those that a mesh axis runs over, the one named last changes fastest.
Arguments:
- tensor: bfloat16 [512, 512, 512], P('ia', 'ja', 'ka'), may hold values from 0 to 122880
- matrix: bfloat16 [512, 32768], P(None, ('ia', 'ja', 'ka')), may hold values from 0 to 4096000
- first_factor: bfloat16 [512, 256], P('ia'), may hold values from 0.05 to 2
- second_factor: bfloat16 [512, 256], P('ja'), may hold values from 0.05 to 2
- time_factor: bfloat16 [512, 256], P('ka'), may hold values from 0.05 to 2
- column_factor: bfloat16 [32768, 256], P(('ia', 'ja', 'ka')), may hold values from 0.05 to 2
Outputs:
- first_new: bfloat16 [512, 256], P('ia')
- second_new: bfloat16 [512, 256], P('ja')
- time_new: bfloat16 [512, 256], P('ka')
All inputs are finite; a program needn't handle non-finite values.
Results may differ from a plain program's by a relative error of at most 0.00075.
The roundings to bfloat16 on the way count: a program that leaves them out, or rounds other values in their place, can miss the bound.
Values may be sent and summed in bfloat16 or wider, within the bound.
No kernel may reach another device: no remote copies, remote signals or barrier semaphores. Data moves between devices by JAX's collectives and lax.ppermute only.
A program may use at most 128 MiB of HBM per device.

v0:
```python
import functools

import jax
import jax.numpy as jnp
from jax import lax
from jax.experimental import pallas as pl
from jax.experimental.pallas import tpu as pltpu
from jax.sharding import PartitionSpec as P


ANY = pl.BlockSpec(memory_space=pl.ANY)
VMEM = pl.BlockSpec(memory_space=pltpu.VMEM)
LIMIT = 32 << 20


def in_hbm(values):
    return pltpu.with_memory_space_constraint(values, pltpu.HBM)


def chunk_of(length, most):
    size = min(length, most)
    while length % size:
        size //= 2
    return size


def kernel_call(kernel, flops, nbytes, **kwargs):
    return pl.pallas_call(
        kernel,
        cost_estimate=pl.CostEstimate(flops=flops, bytes_accessed=nbytes, transcendentals=0),
        compiler_params=pltpu.CompilerParams(vmem_limit_bytes=LIMIT),
        **kwargs,
    )


def bring(sources, targets, sem):
    def copy(index):
        return pltpu.make_async_copy(sources[index], targets[index], sem.at[index])

    for index in range(len(sources)):
        copy(index).start()
    return lambda index: copy(index).wait()


def local_kernel(
    column, second, time, matrix, grams, gram_time, coupled, second_out, time_out, *scratch
):
    f32 = jnp.float32
    held, held_matrix, turned, sem = scratch
    targets = (held, second_out, time_out, held_matrix)
    wait = bring((column, second, time, matrix), targets, sem)
    rank = column.shape[1]
    wait(0)
    turned[...] = held[...].T
    grams[:, :rank] = jnp.dot(turned[...], held[...], preferred_element_type=f32)
    wait(1)
    grams[:, rank:] = jnp.dot(second_out[...].T, second_out[...], preferred_element_type=f32)
    wait(2)
    gram_time[...] = jnp.dot(time_out[...].T, time_out[...], preferred_element_type=f32)
    wait(3)
    coupled[...] = lax.dot_general(
        turned[...], held_matrix[...], (((1,), (1,)), ((), ())), preferred_element_type=f32
    )


def local_products(column, second, time, matrix):
    width, rank = column.shape
    rows = matrix.shape[0]
    f32 = jnp.float32
    return kernel_call(
        local_kernel,
        2 * width * rank * (rank + rows),
        2 * width * (rank + rows),
        out_shape=(
            jax.ShapeDtypeStruct((rank, 2 * rank), f32),
            jax.ShapeDtypeStruct((rank, rank), f32),
            jax.ShapeDtypeStruct((rank, rows), f32),
            jax.ShapeDtypeStruct(second.shape, second.dtype),
            jax.ShapeDtypeStruct(time.shape, time.dtype),
        ),
        in_specs=[ANY] * 4,
        out_specs=(VMEM,) * 5,
        scratch_shapes=[
            pltpu.VMEM(column.shape, column.dtype),
            pltpu.VMEM(matrix.shape, matrix.dtype),
            pltpu.VMEM((rank, width), column.dtype),
            pltpu.SemaphoreType.DMA((4,)),
        ],
    )(*(in_hbm(a) for a in (column, second, time, matrix)))


def slab_kernel(first, chunk, steps, tensor, second, time, *refs):
    *start, total, turned, read, read_sem, ready, ready_sem, added = refs
    ahead = min(4, steps)

    def fetch(step):
        source = tensor.at[:, pl.ds(first + step * chunk, chunk)]
        return pltpu.make_async_copy(source, read.at[step], read_sem.at[step])

    def put(step):
        target = turned.at[pl.ds(step * chunk, chunk)]
        return pltpu.make_async_copy(ready.at[step], target, ready_sem.at[step])

    for step in range(ahead):
        fetch(step).start()
    time_wide = time[...].astype(jnp.float32)
    added[...] = start[0][...] if start else jnp.zeros_like(added)

    def body(step, carry):
        fetch(step).wait()

        @pl.when(step + ahead < steps)
        def _():
            fetch(step + ahead).start()

        block = jnp.swapaxes(read[step], 0, 1)
        for j in range(chunk):
            ready[step, j] = block[j].T
        put(step).start()
        row = pl.multiple_of(first + step * chunk, chunk)
        weights = second[pl.ds(row, chunk), :].astype(jnp.float32)
        khatri = jnp.concatenate(
            [(weights[j : j + 1, :] * time_wide).astype(jnp.bfloat16) for j in range(chunk)], 0
        )
        tiles = jnp.concatenate([block[j] for j in range(chunk)], 1)
        added[...] += jnp.dot(tiles, khatri, preferred_element_type=jnp.float32)
        return carry

    lax.fori_loop(0, steps, body, 0)
    total[...] = added[...].T if start else added[...]

    def finish(step, carry):
        put(step).wait()
        return carry

    lax.fori_loop(0, steps, finish, 0)


def slab_and_turn(tensor, second, time, first, count, start=()):
    tile_i, _, tile_k = tensor.shape
    rank = time.shape[1]
    chunk = chunk_of(count, 8)
    steps = count // chunk
    return kernel_call(
        functools.partial(slab_kernel, first, chunk, steps),
        2 * tile_i * count * tile_k * rank,
        4 * tile_i * count * tile_k,
        out_shape=(
            jax.ShapeDtypeStruct((rank, tile_i) if start else (tile_i, rank), jnp.float32),
            pltpu.HBM((count, tile_k, tile_i), tensor.dtype),
        ),
        in_specs=[ANY] + [VMEM] * (2 + len(start)),
        out_specs=(VMEM, ANY),
        scratch_shapes=[
            pltpu.VMEM((steps, tile_i, chunk, tile_k), tensor.dtype),
            pltpu.SemaphoreType.DMA((steps,)),
            pltpu.VMEM((steps, chunk, tile_k, tile_i), tensor.dtype),
            pltpu.SemaphoreType.DMA((steps,)),
            pltpu.VMEM((tile_i, rank), jnp.float32),
        ],
    )(in_hbm(tensor), second, time, *start)


def fetch_part(parts, which, read, read_sem, chunk):
    steps = read.shape[0]

    def copy(part, step):
        source = parts[part].at[pl.ds(step * chunk, chunk)]
        return pltpu.make_async_copy(source, read.at[step], read_sem.at[step])

    for part in range(len(parts)):

        @pl.when(which[0] == part)
        def _():
            for step in range(steps):
                copy(part, step).start()

    return lambda step: copy(0, step).wait()


def plane_kernel(chunk, parts, which, first_turned, time, total, first, read, read_sem):
    wait = fetch_part(parts, which, read, read_sem, chunk)
    first[...] = first_turned[...].T
    shared = first[...]

    def body(step, carry):
        wait(step)
        sums = []
        for j in range(chunk):
            weighted = jnp.dot(read[step, j], shared, preferred_element_type=jnp.float32)
            scaled = weighted * time[...].astype(jnp.float32)
            sums.append(jnp.sum(scaled, axis=0, keepdims=True))
        row = pl.multiple_of(step * chunk, chunk)
        total[pl.ds(row, chunk), :] = jnp.concatenate(sums, 0)
        return carry

    lax.fori_loop(0, read.shape[0], body, 0)


def time_kernel(chunk, parts, which, first_turned, second, *refs):
    *start, total, first, read, read_sem, wide = refs
    wait = fetch_part(parts, which, read, read_sem, chunk)
    wide[...] = second[...].astype(jnp.float32)
    first[...] = first_turned[...].T
    total[...] = start[0][...] if start else jnp.zeros_like(total)
    shared = first[...]

    def body(step, carry):
        wait(step)
        sums = total[...]
        for j in range(chunk):
            weighted = jnp.dot(read[step, j], shared, preferred_element_type=jnp.float32)
            sums = sums + weighted * wide[pl.ds(step * chunk + j, 1), :]
        total[...] = sums
        return carry

    lax.fori_loop(0, read.shape[0], body, 0)


def weighted_call(kernel, parts, which, args, out_rows, extra=()):
    count, tile_k, tile_i = parts[0].shape
    rank = args[0].shape[0]
    chunk = chunk_of(count, 16)
    steps = count // chunk

    def on_parts(*refs):
        kernel(chunk, refs[: len(parts)], *refs[len(parts) :])

    return kernel_call(
        on_parts,
        2 * tile_i * count * tile_k * rank,
        2 * tile_i * count * tile_k,
        out_shape=jax.ShapeDtypeStruct((out_rows, rank), jnp.float32),
        in_specs=[ANY] * len(parts)
        + [pl.BlockSpec(memory_space=pltpu.SMEM)]
        + [VMEM] * len(args),
        out_specs=VMEM,
        scratch_shapes=[
            pltpu.VMEM((tile_i, rank), args[0].dtype),
            pltpu.VMEM((steps, chunk, tile_k, tile_i), parts[0].dtype),
            pltpu.SemaphoreType.DMA((steps,)),
            *extra,
        ],
    )(*(in_hbm(a) for a in parts), which.reshape(1).astype(jnp.int32), *args)


def cross_product(values):
    return lax.dot_general(
        values, values, (((0,), (0,)), ((), ())), preferred_element_type=jnp.float32
    )


def row_product(values):
    return lax.dot_general(
        values, values, (((1,), (1,)), ((), ())), preferred_element_type=jnp.float32
    )


def swap(values, axis, size, mask):
    return lax.ppermute(values, axis, [(i, i ^ mask) for i in range(size)])


def halve(values, axis, size, mask, dim=0):
    half = values.shape[dim] // 2
    bit = (lax.axis_index(axis) & mask) // mask
    kept = lax.dynamic_slice_in_dim(values, bit * half, half, dim)
    sent = lax.dynamic_slice_in_dim(values, (1 - bit) * half, half, dim)
    return kept + swap(sent, axis, size, mask)


def in_order(own, other, axis, mask):
    bit = (lax.axis_index(axis) & mask) // mask
    return jnp.where(
        bit == 0, jnp.concatenate([own, other], 0), jnp.concatenate([other, own], 0)
    )


def double(values, axis, size, mask):
    return in_order(values, swap(values, axis, size, mask), axis, mask)


def tree_sum(terms):
    while len(terms) > 1:
        terms = [terms[i] + terms[i + 1] for i in range(0, len(terms), 2)]
    return terms[0]


def masks_of(size):
    return [1 << b for b in range(size.bit_length() - 1)]


def spread(values, axis, size, step=1):
    return [values] + [swap(values, axis, size, d) for d in range(step, size, step)]


def all_sum(values, axis, size, step=1):
    return tree_sum(spread(values, axis, size, step))


def full_dot(left, right, dims):
    return lax.dot_general(
        left, right, (dims, ((), ())), precision=lax.Precision.HIGHEST,
        preferred_element_type=jnp.float32,
    )


def on_device(
    size_i, size_j, size_k, tensor, matrix, first_factor, second_factor, time_factor, column_factor
):
    f32 = jnp.float32
    _, tile_j, tile_k = tensor.shape
    rank = first_factor.shape[1]
    share = rank // size_j

    def part_of(place):
        part = 0
        for mask in masks_of(size_j):
            part = 2 * part + (place & mask) // mask
        return part

    part = part_of(lax.axis_index("ja"))

    grams, gram_time, coupled, second_near, time_near = local_products(
        column_factor, second_factor, time_factor, matrix
    )
    for mask in masks_of(size_j):
        grams = halve(grams, "ja", size_j, mask)
    gram_second = grams[:, rank:]
    time_rows = lax.dynamic_slice_in_dim(gram_time, part * share, share, 0)
    grams = jnp.concatenate([grams[:, :rank], time_rows], 1)
    grams = all_sum(grams, "ka", size_k)
    gram_column, time_rows = grams[:, :rank], grams[:, rank:]
    gram_column = all_sum(gram_column, "ia", size_i)
    gram_total = gram_second * time_rows + gram_column
    first_wide = first_factor.astype(f32)
    denominator = full_dot(gram_total, first_wide, ((1,), (1,)))

    for mask in reversed(masks_of(size_i)):
        coupled = halve(coupled, "ia", size_i, mask, 1)
    half = tile_j // 2
    slab, low = slab_and_turn(tensor, second_near, time_near, 0, half)
    slab, high = slab_and_turn(tensor, second_near, time_near, half, half, (slab,))
    turned = (low, high)
    numerator = slab + coupled
    place = lax.axis_index("ja")
    pieces = [lax.dynamic_slice_in_dim(numerator, part * share, share, 0)]
    for d in range(1, size_j):
        sent = lax.dynamic_slice_in_dim(numerator, part_of(place ^ d) * share, share, 0)
        pieces.append(swap(sent, "ja", size_j, d))
    numerator = tree_sum(pieces)
    numerator = all_sum(numerator, "ka", size_k)
    own = lax.dynamic_slice_in_dim(first_wide.T, part * share, share, 0)
    first_new = (own * numerator / denominator).astype(jnp.bfloat16)
    pieces = spread(first_new, "ja", size_j)
    for mask in reversed(masks_of(size_j)):
        pieces = [in_order(pieces[d], pieces[d + mask], "ja", mask) for d in range(mask)]
    first_new = pieces[0]

    firsts = spread(first_new, "ia", size_i)
    gram_first = tree_sum([row_product(piece) for piece in firsts])
    times = time_factor
    for mask in masks_of(size_k):
        times = double(times, "ka", size_k, mask)
    gram_time = cross_product(times)
    upper, *lower = reversed(masks_of(size_i))
    bit = (lax.axis_index("ia") & upper) // upper
    plane_args = ((first_new, time_factor), half)
    sent = weighted_call(plane_kernel, turned, 1 - bit, *plane_args)
    came = swap(sent, "ia", size_i, upper)
    kept = weighted_call(plane_kernel, turned, bit, *plane_args)
    plane_sum = kept + came
    for mask in lower:
        plane_sum = halve(plane_sum, "ia", size_i, mask)
    plane_sum = all_sum(plane_sum, "ka", size_k)
    rows = tile_j // size_i
    own = lax.dynamic_slice_in_dim(second_factor, lax.axis_index("ia") * rows, rows, 0).astype(f32)
    denominator = full_dot(own, gram_first * gram_time, ((1,), (0,)))
    second_new = (own * plane_sum / denominator).astype(jnp.bfloat16)
    for mask in reversed(lower):
        second_new = double(second_new, "ia", size_i, mask)
    other = swap(second_new, "ia", size_i, upper)
    wide = (pltpu.VMEM((half, rank), f32),)
    time_sum = weighted_call(time_kernel, turned, bit, (first_new, second_new), tile_k, wide)
    time_sum = weighted_call(
        time_kernel, turned, 1 - bit, (first_new, other, time_sum), tile_k, wide
    )
    second_new = in_order(second_new, other, "ia", upper)

    seconds = second_new
    for mask in reversed(masks_of(size_j)):
        seconds = double(seconds, "ja", size_j, mask)
    gram_new = cross_product(seconds)
    time_sum = halve(time_sum, "ja", size_j, 1)
    time_sum = all_sum(time_sum, ("ia", "ja"), size_i * size_j, 2)
    rows = tile_k // 2
    own = lax.dynamic_slice_in_dim(
        time_factor, (lax.axis_index("ja") % 2) * rows, rows, 0
    ).astype(f32)
    denominator = full_dot(own, gram_first * gram_new, ((1,), (0,)))
    time_new = (own * time_sum / denominator).astype(jnp.bfloat16)
    time_new = double(time_new, "ja", size_j, 1)
    first_out = first_new.T
    return (first_out, second_new, time_new)


def in_layer(sizes, *args):
    return on_device(*sizes, *args)


def solution(mesh):
    sizes = (mesh.shape["ia"], mesh.shape["ja"], mesh.shape["ka"])
    return jax.shard_map(
        functools.partial(in_layer, sizes),
        mesh=mesh,
        in_specs=(
            P("ia", "ja", "ka"),
            P(None, ("ia", "ja", "ka")),
            P("ia", None),
            P("ja", None),
            P("ka", None),
            P(("ia", "ja", "ka"), None),
        ),
        out_specs=(P("ia", None), P("ja", None), P("ka", None)),
        check_vma=False,
    )
```

profile of v0, /device:TPU:0, one launch (start us, length us, event | category | flops | bytes accessed | tf_op | source)
XLA Modules:
  0.0 89.1 jit_solution(15691731542975833626)
XLA Ops:
  0.6 3.1 %collective-permute-start.21 = (bf16[128,256]{1,0:T(8,128)(2,1)}, bf16[128,256]{1,0:T(8,128)(2,1)S(1)}, u32[]{:S(2)}, u32[]{:S(2)}) collective-permute-start(bf16[128,256]{1,0:T(8,128)(2,1)} %refs_4_.3), channel_id=1, source_target_pairs={{0,1},{1,0},{2,3},{3,2},{4,5},{5,4},{6,7},{7,6},{8,9},{9,8},{10,11... | collective-permute-start | bytes 196616 | tf_op jit(solution)/shard_map/ppermute | solution.py:260
  3.8 2.4 %shard_map.85 = (f32[256,512]{1,0:T(8,128)S(1)}, f32[256,256]{1,0:T(8,128)S(1)}, f32[256,512]{1,0:T(8,128)S(1)}, bf16[128,256]{1,0:T(8,128)(2,1)S(1)}, bf16[128,256]{1,0:T(8,128)(2,1)S(1)}) custom-call(bf16[1024,256]{1,0:T(8,128)(2,1)} %column.1, bf16[128,256]{1,0:T(8,128)(2,1)} %second.1, bf16[128,256]{1,0:T(8,128)(2,1)} %refs_4_.3, bf16[512,1024]{1,0:T(8,128)(2,1)} %matrix.1), custom_call_target="tpu_custom_call" | custom-call | flops 402653184 | bytes 1572864 | tf_op jit(solution)/shard_map/pallas_call | solution.py:70
  6.3 1.6 %collective-permute-start = (f32[256,256]{1,0:T(8,128)S(1)}, f32[256,256]{1,0:T(8,128)S(1)}, u32[]{:S(2)}, u32[]{:S(2)}) collective-permute-start(f32[256,256]{1,0:T(8,128)S(1)} %constant_dynamic-slice_fusion.7), channel_id=1, source_target_pairs={{0,16},{16,0},{1,17},{17,1},{2,18},{18,2},{3,19},{19,3},{4,20},{20... | collective-permute-start | bytes 786440 | tf_op jit(solution)/shard_map/ppermute | solution.py:260
  7.9 4.9 %shard_map.86 = (f32[256,256]{1,0:T(8,128)S(1)}, bf16[64,128,256]{2,1,0:T(8,128)(2,1)}) custom-call(bf16[256,128,128]{2,1,0:T(8,128)(2,1)} %tensor.3, bf16[128,256]{1,0:T(8,128)(2,1)S(1)} %get-tuple-element.12.second, bf16[128,256]{1,0:T(8,128)(2,1)S(1)} %get-tuple-element.13.time), custom_call_target="tpu_custom_call" | custom-call | flops 1073741824 | bytes 8388608 | tf_op jit(solution)/shard_map/pallas_call | solution.py:144
  12.9 5.0 %shard_map.87 = (f32[256,256]{1,0:T(8,128)S(1)}, bf16[64,128,256]{2,1,0:T(8,128)(2,1)}) custom-call(bf16[256,128,128]{2,1,0:T(8,128)(2,1)} %tensor.3, bf16[128,256]{1,0:T(8,128)(2,1)S(1)} %get-tuple-element.12.second, bf16[128,256]{1,0:T(8,128)(2,1)S(1)} %get-tuple-element.13.time, f32[256,256]{1,0:T(8,128)S(1)} %get-tuple-element.14.refs_0_), custom_call_target="tpu_custom_call" | custom-call | flops 1073741824 | bytes 8388608 | tf_op jit(solution)/shard_map/pallas_call | solution.py:144
  18.0 1.6 %collective-permute-start.8 = (f32[64,512]{1,0:T(8,128)S(1)}, f32[64,512]{1,0:T(8,128)S(1)}, u32[]{:S(2)}, u32[]{:S(2)}) collective-permute-start(f32[64,512]{1,0:T(8,128)S(1)} %constant_dynamic-slice_fusion.2), channel_id=1, source_target_pairs={{0,8},{4,12},{8,0},{12,4},{1,9},{5,13},{9,1},{13,5},{2,10},{6,14},... | collective-permute-start | bytes 393224 | tf_op jit(solution)/shard_map/ppermute | solution.py:260
  21.9 2.5 %collective-permute-done.8 = f32[64,512]{1,0:T(8,128)S(1)} collective-permute-done((f32[64,512]{1,0:T(8,128)S(1)}, f32[64,512]{1,0:T(8,128)S(1)}, u32[]{:S(2)}, u32[]{:S(2)}) %collective-permute-start.8) | collective-permute-done | bytes 131104 | tf_op jit(solution)/shard_map/ppermute | solution.py:260
  24.5 2.7 %collective-permute-start.10 = (f32[64,512]{1,0:T(8,128)S(1)}, f32[64,512]{1,0:T(8,128)S(1)}, u32[]{:S(2)}, u32[]{:S(2)}) collective-permute-start(f32[64,512]{1,0:T(8,128)S(1)} %pad_maximum_fusion), channel_id=1, source_target_pairs={{0,2},{1,3},{2,0},{3,1},{4,6},{5,7},{6,4},{7,5},{8,10},{9,11},{10,... | collective-permute-start | bytes 393224 | tf_op jit(solution)/shard_map/ppermute | solution.py:260
  27.1 1.1 %collective-permute-start.11 = (f32[64,512]{1,0:T(8,128)S(1)}, f32[64,512]{1,0:T(8,128)S(1)}, u32[]{:S(2)}, u32[]{:S(2)}) collective-permute-start(f32[64,512]{1,0:T(8,128)S(1)} %pad_maximum_fusion), channel_id=1, source_target_pairs={{0,3},{1,2},{2,1},{3,0},{4,7},{5,6},{6,5},{7,4},{8,11},{9,10},{10,... | collective-permute-start | bytes 393224 | tf_op jit(solution)/shard_map/ppermute | solution.py:260
  28.9 2.7 %collective-permute-start.5 = (f32[64,256]{1,0:T(8,128)S(1)}, f32[64,256]{1,0:T(8,128)S(1)}, u32[]{:S(2)}, u32[]{:S(2)}) collective-permute-start(f32[64,256]{1,0:T(8,128)S(1)} %add_add_fusion.2), channel_id=1, source_target_pairs={{0,2},{1,3},{2,0},{3,1},{4,6},{5,7},{6,4},{7,5},{8,10},{9,11},{10,... | collective-permute-start | bytes 196616 | tf_op jit(solution)/shard_map/ppermute | solution.py:260
  31.6 5.1 %collective-permute-done.10 = f32[64,512]{1,0:T(8,128)S(1)} collective-permute-done((f32[64,512]{1,0:T(8,128)S(1)}, f32[64,512]{1,0:T(8,128)S(1)}, u32[]{:S(2)}, u32[]{:S(2)}) %collective-permute-start.10) | collective-permute-done | bytes 131104 | tf_op jit(solution)/shard_map/ppermute | solution.py:260
  36.8 2.6 %collective-permute-start.6 = (f32[64,256]{1,0:T(8,128)S(1)}, f32[64,256]{1,0:T(8,128)S(1)}, u32[]{:S(2)}, u32[]{:S(2)}) collective-permute-start(f32[64,256]{1,0:T(8,128)S(1)} %add_add_fusion.2), channel_id=1, source_target_pairs={{0,3},{1,2},{2,1},{3,0},{4,7},{5,6},{6,5},{7,4},{8,11},{9,10},{10,... | collective-permute-start | bytes 196616 | tf_op jit(solution)/shard_map/ppermute | solution.py:260
  39.4 2.1 %collective-permute-start.4 = (f32[64,256]{1,0:T(8,128)S(1)}, f32[64,256]{1,0:T(8,128)S(1)}, u32[]{:S(2)}, u32[]{:S(2)}) collective-permute-start(f32[64,256]{1,0:T(8,128)S(1)} %add_add_fusion.2), channel_id=1, source_target_pairs={{0,1},{1,0},{2,3},{3,2},{4,5},{5,4},{6,7},{7,6},{8,9},{9,8},{10,11... | collective-permute-start | bytes 196616 | tf_op jit(solution)/shard_map/ppermute | solution.py:260
  42.1 1.0 %collective-permute-done.6 = f32[64,256]{1,0:T(8,128)S(1)} collective-permute-done((f32[64,256]{1,0:T(8,128)S(1)}, f32[64,256]{1,0:T(8,128)S(1)}, u32[]{:S(2)}, u32[]{:S(2)}) %collective-permute-start.6) | collective-permute-done | bytes 65568 | tf_op jit(solution)/shard_map/ppermute | solution.py:260
  43.8 2.1 %collective-permute-done.12 = f32[64,256]{1,0:T(8,128)S(1)} collective-permute-done((f32[64,256]{1,0:T(8,128)S(1)}, f32[64,256]{1,0:T(8,128)S(1)}, u32[]{:S(2)}, u32[]{:S(2)}) %collective-permute-start.12) | collective-permute-done | bytes 65568 | tf_op jit(solution)/shard_map/ppermute | solution.py:260
  46.2 1.6 %collective-permute-start.13 = (bf16[64,256]{1,0:T(8,128)(2,1)S(1)}, bf16[64,256]{1,0:T(8,128)(2,1)S(1)}, u32[]{:S(2)}, u32[]{:S(2)}) collective-permute-start(bf16[64,256]{1,0:T(8,128)(2,1)S(1)} %fusion.17), channel_id=1, source_target_pairs={{0,8},{4,12},{8,0},{12,4},{1,9},{5,13},{9,1},{13,5},{2,10},{6,14},... | collective-permute-start | bytes 98312 | tf_op jit(solution)/shard_map/ppermute | solution.py:260
  47.8 1.2 %collective-permute-start.22 = (bf16[256,256]{1,0:T(8,128)(2,1)S(1)}, bf16[256,256]{1,0:T(8,128)(2,1)S(1)}, u32[]{:S(2)}, u32[]{:S(2)}) collective-permute-start(bf16[256,256]{1,0:T(8,128)(2,1)S(1)} %maximum_select_fusion.5), channel_id=1, source_target_pairs={{0,2},{1,3},{2,0},{3,1},{4,6},{5,7},{6,4},{7,5},{8,10},{9,11},{10,... | collective-permute-start | bytes 393224 | tf_op jit(solution)/shard_map/ppermute | solution.py:260
  50.2 2.2 %collective-permute-done.15 = bf16[64,256]{1,0:T(8,128)(2,1)S(1)} collective-permute-done((bf16[64,256]{1,0:T(8,128)(2,1)S(1)}, bf16[64,256]{1,0:T(8,128)(2,1)S(1)}, u32[]{:S(2)}, u32[]{:S(2)}) %collective-permute-start.15) | collective-permute-done | bytes 32800 | tf_op jit(solution)/shard_map/ppermute | solution.py:260
  53.2 3.1 %shard_map.89 = f32[64,256]{1,0:T(8,128)S(1)} custom-call(bf16[64,128,256]{2,1,0:T(8,128)(2,1)} %get-tuple-element.19.refs_0_, bf16[64,128,256]{2,1,0:T(8,128)(2,1)} %get-tuple-element.20.refs_1_, s32[1]{0:T(128)} %bitcast.3.refs_2_, bf16[256,256]{1,0:T(8,128)(2,1)S(1)} %maximum_select_fusion.4.refs_3_, bf16[128,256]{1,0:T(8,128)(2,1)S(1)} %copy-done.1), custom_call_target="tpu_custom_call" | custom-call | flops 1073741824 | bytes 4194304 | tf_op jit(solution)/shard_map/pallas_call | solution.py:229
  56.4 1.5 %collective-permute-start.16 = (f32[64,256]{1,0:T(8,128)S(1)}, f32[64,256]{1,0:T(8,128)S(1)}, u32[]{:S(2)}, u32[]{:S(2)}) collective-permute-start(f32[64,256]{1,0:T(8,128)S(1)} %shard_map.89), channel_id=1, source_target_pairs={{0,16},{16,0},{1,17},{17,1},{2,18},{18,2},{3,19},{19,3},{4,20},{20... | collective-permute-start | bytes 196616 | tf_op jit(solution)/shard_map/ppermute | solution.py:260
  57.9 3.2 %shard_map.88 = f32[64,256]{1,0:T(8,128)S(1)} custom-call(bf16[64,128,256]{2,1,0:T(8,128)(2,1)} %get-tuple-element.19.refs_0_, bf16[64,128,256]{2,1,0:T(8,128)(2,1)} %get-tuple-element.20.refs_1_, s32[1]{0:T(128)} %bitcast.2.refs_2_, bf16[256,256]{1,0:T(8,128)(2,1)S(1)} %maximum_select_fusion.4.refs_3_, bf16[128,256]{1,0:T(8,128)(2,1)S(1)} %copy-done.1), custom_call_target="tpu_custom_call" | custom-call | flops 1073741824 | bytes 4194304 | tf_op jit(solution)/shard_map/pallas_call | solution.py:229
  61.1 1.8 %collective-permute-start.18 = (f32[64,256]{1,0:T(8,128)S(1)}, f32[64,256]{1,0:T(8,128)S(1)}, u32[]{:S(2)}, u32[]{:S(2)}) collective-permute-start(f32[64,256]{1,0:T(8,128)S(1)} %add.173), channel_id=1, source_target_pairs={{0,2},{1,3},{2,0},{3,1},{4,6},{5,7},{6,4},{7,5},{8,10},{9,11},{10,... | collective-permute-start | bytes 196616 | tf_op jit(solution)/shard_map/ppermute | solution.py:260
  63.0 2.6 %collective-permute-start.19 = (f32[64,256]{1,0:T(8,128)S(1)}, f32[64,256]{1,0:T(8,128)S(1)}, u32[]{:S(2)}, u32[]{:S(2)}) collective-permute-start(f32[64,256]{1,0:T(8,128)S(1)} %add.173), channel_id=1, source_target_pairs={{0,3},{1,2},{2,1},{3,0},{4,7},{5,6},{6,5},{7,4},{8,11},{9,10},{10,... | collective-permute-start | bytes 196616 | tf_op jit(solution)/shard_map/ppermute | solution.py:260
  66.9 2.1 %collective-permute-done.19 = f32[64,256]{1,0:T(8,128)S(1)} collective-permute-done((f32[64,256]{1,0:T(8,128)S(1)}, f32[64,256]{1,0:T(8,128)S(1)}, u32[]{:S(2)}, u32[]{:S(2)}) %collective-permute-start.19) | collective-permute-done | bytes 65568 | tf_op jit(solution)/shard_map/ppermute | solution.py:260
  69.9 1.1 %collective-permute-start.23 = (bf16[64,256]{1,0:T(8,128)(2,1)S(1)}, bf16[64,256]{1,0:T(8,128)(2,1)S(1)}, u32[]{:S(2)}, u32[]{:S(2)}) collective-permute-start(bf16[64,256]{1,0:T(8,128)(2,1)S(1)} %divide_convert_fusion.1.refs_4_), channel_id=1, source_target_pairs={{0,16},{16,0},{1,17},{17,1},{2,18},{18,2},{3,19},{19,3},{4,20},{20... | collective-permute-start | bytes 98312 | tf_op jit(solution)/shard_map/ppermute | solution.py:260
  71.0 3.1 %shard_map.90.refs_5_ = f32[128,256]{1,0:T(8,128)S(1)} custom-call(bf16[64,128,256]{2,1,0:T(8,128)(2,1)} %get-tuple-element.19.refs_0_, bf16[64,128,256]{2,1,0:T(8,128)(2,1)} %get-tuple-element.20.refs_1_, s32[1]{0:T(128)} %bitcast.2.refs_2_, bf16[256,256]{1,0:T(8,128)(2,1)S(1)} %maximum_select_fusion.4.refs_3_, bf16[64,256]{1,0:T(8,128)(2,1)S(1)} %divide_convert_fusion.1.refs_4_), custom_call_target="tpu_custom_call" | custom-call | flops 1073741824 | bytes 4194304 | tf_op jit(solution)/shard_map/pallas_call | solution.py:229
  74.2 1.0 %collective-permute-start.28 = (bf16[128,256]{1,0:T(8,128)(2,1)S(1)}, bf16[128,256]{1,0:T(8,128)(2,1)S(1)}, u32[]{:S(2)}, u32[]{:S(2)}) collective-permute-start(bf16[128,256]{1,0:T(8,128)(2,1)S(1)} %maximum_select_fusion.9), channel_id=1, source_target_pairs={{0,8},{4,12},{8,0},{12,4},{1,9},{5,13},{9,1},{13,5},{2,10},{6,14},... | collective-permute-start | bytes 196616 | tf_op jit(solution)/shard_map/ppermute | solution.py:260
  75.1 3.1 %shard_map.91 = f32[128,256]{1,0:T(8,128)S(1)} custom-call(bf16[64,128,256]{2,1,0:T(8,128)(2,1)} %get-tuple-element.19.refs_0_, bf16[64,128,256]{2,1,0:T(8,128)(2,1)} %get-tuple-element.20.refs_1_, s32[1]{0:T(128)} %bitcast.3.refs_2_, bf16[256,256]{1,0:T(8,128)(2,1)S(1)} %maximum_select_fusion.4.refs_3_, ...), custom_call_target="tpu_custom_call" | custom-call | flops 1073741824 | bytes 4194304 | tf_op jit(solution)/shard_map/pallas_call | solution.py:229
  79.6 1.3 %collective-permute-start.26 = (f32[64,256]{1,0:T(8,128)S(1)}, f32[64,256]{1,0:T(8,128)S(1)}, u32[]{:S(2)}, u32[]{:S(2)}) collective-permute-start(f32[64,256]{1,0:T(8,128)S(1)} %dynamic-slice_add_fusion.2), channel_id=1, source_target_pairs={{0,16},{4,20},{8,24},{12,28},{16,0},{20,4},{24,8},{28,12},{1,17},{... | collective-permute-start | bytes 196616 | tf_op jit(solution)/shard_map/ppermute | solution.py:260
  80.9 1.4 %collective-permute-start.27 = (f32[64,256]{1,0:T(8,128)S(1)}, f32[64,256]{1,0:T(8,128)S(1)}, u32[]{:S(2)}, u32[]{:S(2)}) collective-permute-start(f32[64,256]{1,0:T(8,128)S(1)} %dynamic-slice_add_fusion.2), channel_id=1, source_target_pairs={{0,24},{4,28},{8,16},{12,20},{16,8},{20,12},{24,0},{28,4},{1,25},{... | collective-permute-start | bytes 196616 | tf_op jit(solution)/shard_map/ppermute | solution.py:260
  84.2 1.8 %collective-permute-done.27 = f32[64,256]{1,0:T(8,128)S(1)} collective-permute-done((f32[64,256]{1,0:T(8,128)S(1)}, f32[64,256]{1,0:T(8,128)S(1)}, u32[]{:S(2)}, u32[]{:S(2)}) %collective-permute-start.27) | collective-permute-done | bytes 65568 | tf_op jit(solution)/shard_map/ppermute | solution.py:260
  86.0 1.1 %collective-permute-done.25 = f32[64,256]{1,0:T(8,128)S(1)} collective-permute-done((f32[64,256]{1,0:T(8,128)S(1)}, f32[64,256]{1,0:T(8,128)S(1)}, u32[]{:S(2)}, u32[]{:S(2)}) %collective-permute-start.25) | collective-permute-done | bytes 65568 | tf_op jit(solution)/shard_map/ppermute | solution.py:260
  (80 shorter events, 14.2 us)
Async XLA Ops:
  0.6 41.2 %copy-start = (bf16[256,256]{1,0:T(8,128)(2,1)S(1)}, bf16[256,256]{1,0:T(8,128)(2,1)}, u32[]{:S(2)}) copy-start(bf16[256,256]{1,0:T(8,128)(2,1)} %param.8) | copy-start | bytes 393220
  0.6 47.1 %collective-permute-start.21 = (bf16[128,256]{1,0:T(8,128)(2,1)}, bf16[128,256]{1,0:T(8,128)(2,1)S(1)}, u32[]{:S(2)}, u32[]{:S(2)}) collective-permute-start(bf16[128,256]{1,0:T(8,128)(2,1)} %refs_4_.3), channel_id=1, source_target_pairs={{0,1},{1,0},{2,3},{3,2},{4,5},{5,4},{6,7},{7,6},{8,9},{9,8},{10,11... | collective-permute-start | bytes 196616 | tf_op jit(solution)/shard_map/ppermute | solution.py:260
  6.2 11.7 %collective-permute-start.7 = (f32[128,512]{1,0:T(8,128)S(1)}, f32[128,512]{1,0:T(8,128)S(1)}, u32[]{:S(2)}, u32[]{:S(2)}) collective-permute-start(f32[128,512]{1,0:T(8,128)S(1)} %constant_dynamic-slice_fusion.3), channel_id=1, source_target_pairs={{0,4},{4,0},{8,12},{12,8},{1,5},{5,1},{9,13},{13,9},{2,6},{6,2},{1... | collective-permute-start | bytes 786440 | tf_op jit(solution)/shard_map/ppermute | solution.py:260
  6.3 13.3 %collective-permute-start = (f32[256,256]{1,0:T(8,128)S(1)}, f32[256,256]{1,0:T(8,128)S(1)}, u32[]{:S(2)}, u32[]{:S(2)}) collective-permute-start(f32[256,256]{1,0:T(8,128)S(1)} %constant_dynamic-slice_fusion.7), channel_id=1, source_target_pairs={{0,16},{16,0},{1,17},{17,1},{2,18},{18,2},{3,19},{19,3},{4,20},{20... | collective-permute-start | bytes 786440 | tf_op jit(solution)/shard_map/ppermute | solution.py:260
  18.0 6.4 %collective-permute-start.8 = (f32[64,512]{1,0:T(8,128)S(1)}, f32[64,512]{1,0:T(8,128)S(1)}, u32[]{:S(2)}, u32[]{:S(2)}) collective-permute-start(f32[64,512]{1,0:T(8,128)S(1)} %constant_dynamic-slice_fusion.2), channel_id=1, source_target_pairs={{0,8},{4,12},{8,0},{12,4},{1,9},{5,13},{9,1},{13,5},{2,10},{6,14},... | collective-permute-start | bytes 393224 | tf_op jit(solution)/shard_map/ppermute | solution.py:260
  19.7 7.5 %collective-permute-start.2 = (f32[64,256]{1,0:T(8,128)S(1)}, f32[64,256]{1,0:T(8,128)S(1)}, u32[]{:S(2)}, u32[]{:S(2)}) collective-permute-start(f32[64,256]{1,0:T(8,128)S(1)} %get-tuple-element.26), channel_id=1, source_target_pairs={{0,8},{4,12},{8,0},{12,4},{1,9},{5,13},{9,1},{13,5},{2,10},{6,14},... | collective-permute-start | bytes 196616 | tf_op jit(solution)/shard_map/ppermute | solution.py:260
  20.2 8.0 %collective-permute-start.3 = (f32[64,256]{1,0:T(8,128)S(1)}, f32[64,256]{1,0:T(8,128)S(1)}, u32[]{:S(2)}, u32[]{:S(2)}) collective-permute-start(f32[64,256]{1,0:T(8,128)S(1)} %get-tuple-element.25), channel_id=1, source_target_pairs={{0,12},{4,8},{8,4},{12,0},{1,13},{5,9},{9,5},{13,1},{2,14},{6,10},... | collective-permute-start | bytes 196616 | tf_op jit(solution)/shard_map/ppermute | solution.py:260
  21.0 7.9 %collective-permute-start.1 = (f32[64,256]{1,0:T(8,128)S(1)}, f32[64,256]{1,0:T(8,128)S(1)}, u32[]{:S(2)}, u32[]{:S(2)}) collective-permute-start(f32[64,256]{1,0:T(8,128)S(1)} %get-tuple-element.24), channel_id=1, source_target_pairs={{0,4},{4,0},{8,12},{12,8},{1,5},{5,1},{9,13},{13,9},{2,6},{6,2},{1... | collective-permute-start | bytes 196616 | tf_op jit(solution)/shard_map/ppermute | solution.py:260
  24.5 12.3 %collective-permute-start.10 = (f32[64,512]{1,0:T(8,128)S(1)}, f32[64,512]{1,0:T(8,128)S(1)}, u32[]{:S(2)}, u32[]{:S(2)}) collective-permute-start(f32[64,512]{1,0:T(8,128)S(1)} %pad_maximum_fusion), channel_id=1, source_target_pairs={{0,2},{1,3},{2,0},{3,1},{4,6},{5,7},{6,4},{7,5},{8,10},{9,11},{10,... | collective-permute-start | bytes 393224 | tf_op jit(solution)/shard_map/ppermute | solution.py:260
  27.1 12.3 %collective-permute-start.11 = (f32[64,512]{1,0:T(8,128)S(1)}, f32[64,512]{1,0:T(8,128)S(1)}, u32[]{:S(2)}, u32[]{:S(2)}) collective-permute-start(f32[64,512]{1,0:T(8,128)S(1)} %pad_maximum_fusion), channel_id=1, source_target_pairs={{0,3},{1,2},{2,1},{3,0},{4,7},{5,6},{6,5},{7,4},{8,11},{9,10},{10,... | collective-permute-start | bytes 393224 | tf_op jit(solution)/shard_map/ppermute | solution.py:260
  28.2 13.3 %collective-permute-start.9 = (f32[64,512]{1,0:T(8,128)S(1)}, f32[64,512]{1,0:T(8,128)S(1)}, u32[]{:S(2)}, u32[]{:S(2)}) collective-permute-start(f32[64,512]{1,0:T(8,128)S(1)} %pad_maximum_fusion), channel_id=1, source_target_pairs={{0,1},{1,0},{2,3},{3,2},{4,5},{5,4},{6,7},{7,6},{8,9},{9,8},{10,11... | collective-permute-start | bytes 393224 | tf_op jit(solution)/shard_map/ppermute | solution.py:260
  28.9 13.1 %collective-permute-start.5 = (f32[64,256]{1,0:T(8,128)S(1)}, f32[64,256]{1,0:T(8,128)S(1)}, u32[]{:S(2)}, u32[]{:S(2)}) collective-permute-start(f32[64,256]{1,0:T(8,128)S(1)} %add_add_fusion.2), channel_id=1, source_target_pairs={{0,2},{1,3},{2,0},{3,1},{4,6},{5,7},{6,4},{7,5},{8,10},{9,11},{10,... | collective-permute-start | bytes 196616 | tf_op jit(solution)/shard_map/ppermute | solution.py:260
  36.8 6.3 %collective-permute-start.6 = (f32[64,256]{1,0:T(8,128)S(1)}, f32[64,256]{1,0:T(8,128)S(1)}, u32[]{:S(2)}, u32[]{:S(2)}) collective-permute-start(f32[64,256]{1,0:T(8,128)S(1)} %add_add_fusion.2), channel_id=1, source_target_pairs={{0,3},{1,2},{2,1},{3,0},{4,7},{5,6},{6,5},{7,4},{8,11},{9,10},{10,... | collective-permute-start | bytes 196616 | tf_op jit(solution)/shard_map/ppermute | solution.py:260
  39.4 4.4 %collective-permute-start.4 = (f32[64,256]{1,0:T(8,128)S(1)}, f32[64,256]{1,0:T(8,128)S(1)}, u32[]{:S(2)}, u32[]{:S(2)}) collective-permute-start(f32[64,256]{1,0:T(8,128)S(1)} %add_add_fusion.2), channel_id=1, source_target_pairs={{0,1},{1,0},{2,3},{3,2},{4,5},{5,4},{6,7},{7,6},{8,9},{9,8},{10,11... | collective-permute-start | bytes 196616 | tf_op jit(solution)/shard_map/ppermute | solution.py:260
  41.6 4.3 %collective-permute-start.12 = (f32[64,256]{1,0:T(8,128)S(1)}, f32[64,256]{1,0:T(8,128)S(1)}, u32[]{:S(2)}, u32[]{:S(2)}) collective-permute-start(f32[64,256]{1,0:T(8,128)S(1)} %slice.19), channel_id=1, source_target_pairs={{0,16},{16,0},{1,17},{17,1},{2,18},{18,2},{3,19},{19,3},{4,20},{20... | collective-permute-start | bytes 196616 | tf_op jit(solution)/shard_map/ppermute | solution.py:260
  46.2 4.0 %collective-permute-start.13 = (bf16[64,256]{1,0:T(8,128)(2,1)S(1)}, bf16[64,256]{1,0:T(8,128)(2,1)S(1)}, u32[]{:S(2)}, u32[]{:S(2)}) collective-permute-start(bf16[64,256]{1,0:T(8,128)(2,1)S(1)} %fusion.17), channel_id=1, source_target_pairs={{0,8},{4,12},{8,0},{12,4},{1,9},{5,13},{9,1},{13,5},{2,10},{6,14},... | collective-permute-start | bytes 98312 | tf_op jit(solution)/shard_map/ppermute | solution.py:260
  47.8 18.0 %collective-permute-start.22 = (bf16[256,256]{1,0:T(8,128)(2,1)S(1)}, bf16[256,256]{1,0:T(8,128)(2,1)S(1)}, u32[]{:S(2)}, u32[]{:S(2)}) collective-permute-start(bf16[256,256]{1,0:T(8,128)(2,1)S(1)} %maximum_select_fusion.5), channel_id=1, source_target_pairs={{0,2},{1,3},{2,0},{3,1},{4,6},{5,7},{6,4},{7,5},{8,10},{9,11},{10,... | collective-permute-start | bytes 393224 | tf_op jit(solution)/shard_map/ppermute | solution.py:260
  49.0 3.3 %collective-permute-start.15 = (bf16[64,256]{1,0:T(8,128)(2,1)S(1)}, bf16[64,256]{1,0:T(8,128)(2,1)S(1)}, u32[]{:S(2)}, u32[]{:S(2)}) collective-permute-start(bf16[64,256]{1,0:T(8,128)(2,1)S(1)} %fusion.17), channel_id=1, source_target_pairs={{0,12},{4,8},{8,4},{12,0},{1,13},{5,9},{9,5},{13,1},{2,14},{6,10},... | collective-permute-start | bytes 98312 | tf_op jit(solution)/shard_map/ppermute | solution.py:260
  49.0 3.3 %collective-permute-start.14 = (bf16[64,256]{1,0:T(8,128)(2,1)S(1)}, bf16[64,256]{1,0:T(8,128)(2,1)S(1)}, u32[]{:S(2)}, u32[]{:S(2)}) collective-permute-start(bf16[64,256]{1,0:T(8,128)(2,1)S(1)} %fusion.17), channel_id=1, source_target_pairs={{0,4},{4,0},{8,12},{12,8},{1,5},{5,1},{9,13},{13,9},{2,6},{6,2},{1... | collective-permute-start | bytes 98312 | tf_op jit(solution)/shard_map/ppermute | solution.py:260
  52.7 12.9 %collective-permute-start.20 = (bf16[256,256]{1,0:T(8,128)(2,1)S(1)}, bf16[256,256]{1,0:T(8,128)(2,1)S(1)}, u32[]{:S(2)}, u32[]{:S(2)}) collective-permute-start(bf16[256,256]{1,0:T(8,128)(2,1)S(1)} %maximum_select_fusion.4.refs_3_), channel_id=1, source_target_pairs={{0,16},{16,0},{1,17},{17,1},{2,18},{18,2},{3,19},{19,3},{4,20},{20... | collective-permute-start | bytes 393224 | tf_op jit(solution)/shard_map/ppermute | solution.py:260
  56.4 4.7 %collective-permute-start.16 = (f32[64,256]{1,0:T(8,128)S(1)}, f32[64,256]{1,0:T(8,128)S(1)}, u32[]{:S(2)}, u32[]{:S(2)}) collective-permute-start(f32[64,256]{1,0:T(8,128)S(1)} %shard_map.89), channel_id=1, source_target_pairs={{0,16},{16,0},{1,17},{17,1},{2,18},{18,2},{3,19},{19,3},{4,20},{20... | collective-permute-start | bytes 196616 | tf_op jit(solution)/shard_map/ppermute | solution.py:260
  61.1 5.8 %collective-permute-start.18 = (f32[64,256]{1,0:T(8,128)S(1)}, f32[64,256]{1,0:T(8,128)S(1)}, u32[]{:S(2)}, u32[]{:S(2)}) collective-permute-start(f32[64,256]{1,0:T(8,128)S(1)} %add.173), channel_id=1, source_target_pairs={{0,2},{1,3},{2,0},{3,1},{4,6},{5,7},{6,4},{7,5},{8,10},{9,11},{10,... | collective-permute-start | bytes 196616 | tf_op jit(solution)/shard_map/ppermute | solution.py:260
  63.0 6.1 %collective-permute-start.19 = (f32[64,256]{1,0:T(8,128)S(1)}, f32[64,256]{1,0:T(8,128)S(1)}, u32[]{:S(2)}, u32[]{:S(2)}) collective-permute-start(f32[64,256]{1,0:T(8,128)S(1)} %add.173), channel_id=1, source_target_pairs={{0,3},{1,2},{2,1},{3,0},{4,7},{5,6},{6,5},{7,4},{8,11},{9,10},{10,... | collective-permute-start | bytes 196616 | tf_op jit(solution)/shard_map/ppermute | solution.py:260
  65.6 4.3 %collective-permute-start.17 = (f32[64,256]{1,0:T(8,128)S(1)}, f32[64,256]{1,0:T(8,128)S(1)}, u32[]{:S(2)}, u32[]{:S(2)}) collective-permute-start(f32[64,256]{1,0:T(8,128)S(1)} %add.173), channel_id=1, source_target_pairs={{0,1},{1,0},{2,3},{3,2},{4,5},{5,4},{6,7},{7,6},{8,9},{9,8},{10,11... | collective-permute-start | bytes 196616 | tf_op jit(solution)/shard_map/ppermute | solution.py:260
  69.9 4.2 %collective-permute-start.23 = (bf16[64,256]{1,0:T(8,128)(2,1)S(1)}, bf16[64,256]{1,0:T(8,128)(2,1)S(1)}, u32[]{:S(2)}, u32[]{:S(2)}) collective-permute-start(bf16[64,256]{1,0:T(8,128)(2,1)S(1)} %divide_convert_fusion.1.refs_4_), channel_id=1, source_target_pairs={{0,16},{16,0},{1,17},{17,1},{2,18},{18,2},{3,19},{19,3},{4,20},{20... | collective-permute-start | bytes 98312 | tf_op jit(solution)/shard_map/ppermute | solution.py:260
  74.2 4.3 %collective-permute-start.28 = (bf16[128,256]{1,0:T(8,128)(2,1)S(1)}, bf16[128,256]{1,0:T(8,128)(2,1)S(1)}, u32[]{:S(2)}, u32[]{:S(2)}) collective-permute-start(bf16[128,256]{1,0:T(8,128)(2,1)S(1)} %maximum_select_fusion.9), channel_id=1, source_target_pairs={{0,8},{4,12},{8,0},{12,4},{1,9},{5,13},{9,1},{13,5},{2,10},{6,14},... | collective-permute-start | bytes 196616 | tf_op jit(solution)/shard_map/ppermute | solution.py:260
  78.2 1.3 %collective-permute-start.24 = (f32[64,256]{1,0:T(8,128)S(1)}, f32[64,256]{1,0:T(8,128)S(1)}, u32[]{:S(2)}, u32[]{:S(2)}) collective-permute-start(f32[64,256]{1,0:T(8,128)S(1)} %constant_dynamic-slice_fusion), channel_id=1, source_target_pairs={{0,4},{4,0},{8,12},{12,8},{1,5},{5,1},{9,13},{13,9},{2,6},{6,2},{1... | collective-permute-start | bytes 196616 | tf_op jit(solution)/shard_map/ppermute | solution.py:260
  78.5 4.6 %collective-permute-start.29 = (bf16[256,256]{1,0:T(8,128)(2,1)S(1)}, bf16[256,256]{1,0:T(8,128)(2,1)S(1)}, u32[]{:S(2)}, u32[]{:S(2)}) collective-permute-start(bf16[256,256]{1,0:T(8,128)(2,1)S(1)} %maximum_select_fusion.6), channel_id=1, source_target_pairs={{0,4},{4,0},{8,12},{12,8},{1,5},{5,1},{9,13},{13,9},{2,6},{6,2},{1... | collective-permute-start | bytes 393224 | tf_op jit(solution)/shard_map/ppermute | solution.py:260
  79.6 4.6 %collective-permute-start.26 = (f32[64,256]{1,0:T(8,128)S(1)}, f32[64,256]{1,0:T(8,128)S(1)}, u32[]{:S(2)}, u32[]{:S(2)}) collective-permute-start(f32[64,256]{1,0:T(8,128)S(1)} %dynamic-slice_add_fusion.2), channel_id=1, source_target_pairs={{0,16},{4,20},{8,24},{12,28},{16,0},{20,4},{24,8},{28,12},{1,17},{... | collective-permute-start | bytes 196616 | tf_op jit(solution)/shard_map/ppermute | solution.py:260
  80.9 5.2 %collective-permute-start.27 = (f32[64,256]{1,0:T(8,128)S(1)}, f32[64,256]{1,0:T(8,128)S(1)}, u32[]{:S(2)}, u32[]{:S(2)}) collective-permute-start(f32[64,256]{1,0:T(8,128)S(1)} %dynamic-slice_add_fusion.2), channel_id=1, source_target_pairs={{0,24},{4,28},{8,16},{12,20},{16,8},{20,12},{24,0},{28,4},{1,25},{... | collective-permute-start | bytes 196616 | tf_op jit(solution)/shard_map/ppermute | solution.py:260
  82.2 4.9 %collective-permute-start.25 = (f32[64,256]{1,0:T(8,128)S(1)}, f32[64,256]{1,0:T(8,128)S(1)}, u32[]{:S(2)}, u32[]{:S(2)}) collective-permute-start(f32[64,256]{1,0:T(8,128)S(1)} %dynamic-slice_add_fusion.2), channel_id=1, source_target_pairs={{0,8},{4,12},{8,0},{12,4},{16,24},{20,28},{24,16},{28,20},{1,9},{5... | collective-permute-start | bytes 196616 | tf_op jit(solution)/shard_map/ppermute | solution.py:260
  87.2 1.3 %collective-permute-start.30 = (bf16[64,256]{1,0:T(8,128)(2,1)S(1)}, bf16[64,256]{1,0:T(8,128)(2,1)S(1)}, u32[]{:S(2)}, u32[]{:S(2)}) collective-permute-start(bf16[64,256]{1,0:T(8,128)(2,1)S(1)} %divide_convert_fusion), channel_id=1, source_target_pairs={{0,4},{4,0},{8,12},{12,8},{1,5},{5,1},{9,13},{13,9},{2,6},{6,2},{1... | collective-permute-start | bytes 98312 | tf_op jit(solution)/shard_map/ppermute | solution.py:260
  (3 other events, 42.5 us)
where the time goes:
time: 89.3 us; the launch traced here: 89.1 us
  starting transfers between devices  36.8 us (41%)
  Pallas kernels  24.7 us (28%)
  waiting for transfers between devices  22.5 us (25%)
  matrix products  1.76 us (2%)
  between operations  1.16 us (1%)
  local copies, waits for them, and re-layouts  1.1 us (1%)
  other arithmetic  1.04 us (1%)
    ppermute x31, starting transfers between devices, swap(): return lax.ppermute(values, axis, [(i, i ^ mask) for i in range(size)])  36.8 us
    ppermute x31, waiting for transfers between devices, swap(): return lax.ppermute(values, axis, [(i, i ^ mask) for i in range(size)])  22.5 us
    pallas_call x4, Pallas kernels, weighted_call(): kernel_call(on_parts, 2 * tile_i * count * tile_k * rank, 2 * tile_i * co...  12.5 us
    pallas_call x2, Pallas kernels, slab_and_turn(): kernel_call(functools.partial(slab_kernel, first, chunk, steps), 2 * tile...  9.86 us
    pallas_call x1, Pallas kernels, local_products(): kernel_call(local_kernel, 2 * width * rank * (rank + rows), 2 * width * (...  2.4 us
  transfers between devices with their start and end apart: 31, of which 16 were waited for; matrix products, arithmetic and copies ran while one was open for 4% of the time, Pallas kernels for 28%

commit v1 on v0

--- a/solution.py
+++ b/solution.py
@@ -297,6 +297,13 @@
     return tree_sum(spread(values, axis, size, step))
 
 
+def far_sum(values, axis, size):
+    terms = [values]
+    for d in range(1, size):
+        terms.append(swap(values, axis, size, d))
+    return tree_sum(terms)
+
+
 def full_dot(left, right, dims):
     return lax.dot_general(
         left, right, (dims, ((), ())), precision=lax.Precision.HIGHEST,
@@ -328,7 +335,7 @@
     gram_second = grams[:, rank:]
     time_rows = lax.dynamic_slice_in_dim(gram_time, part * share, share, 0)
     grams = jnp.concatenate([grams[:, :rank], time_rows], 1)
-    grams = all_sum(grams, "ka", size_k)
+    grams = far_sum(grams, "ka", size_k)
     gram_column, time_rows = grams[:, :rank], grams[:, rank:]
     gram_column = all_sum(gram_column, "ia", size_i)
     gram_total = gram_second * time_rows + gram_column
@@ -348,7 +355,7 @@
         sent = lax.dynamic_slice_in_dim(numerator, part_of(place ^ d) * share, share, 0)
         pieces.append(swap(sent, "ja", size_j, d))
     numerator = tree_sum(pieces)
-    numerator = all_sum(numerator, "ka", size_k)
+    numerator = far_sum(numerator, "ka", size_k)
     own = lax.dynamic_slice_in_dim(first_wide.T, part * share, share, 0)
     first_new = (own * numerator / denominator).astype(jnp.bfloat16)
     pieces = spread(first_new, "ja", size_j)
@@ -371,7 +378,7 @@
     plane_sum = kept + came
     for mask in lower:
         plane_sum = halve(plane_sum, "ia", size_i, mask)
-    plane_sum = all_sum(plane_sum, "ka", size_k)
+    plane_sum = far_sum(plane_sum, "ka", size_k)
     rows = tile_j // size_i
     own = lax.dynamic_slice_in_dim(second_factor, lax.axis_index("ia") * rows, rows, 0).astype(f32)
     denominator = full_dot(own, gram_first * gram_time, ((1,), (0,)))

time: 89.3 us -> 89.3 us (level)
  no operation moved by 1% of the time
where the time goes in v1:
time: 89.3 us; the launch traced here: 89.1 us
  starting transfers between devices  36.8 us (41%)
  Pallas kernels  24.7 us (28%)
  waiting for transfers between devices  22.5 us (25%)
  matrix products  1.76 us (2%)
  between operations  1.16 us (1%)
  local copies, waits for them, and re-layouts  1.1 us (1%)
  other arithmetic  1.04 us (1%)
    ppermute x31, starting transfers between devices, swap(): return lax.ppermute(values, axis, [(i, i ^ mask) for i in range(size)])  36.8 us
    ppermute x31, waiting for transfers between devices, swap(): return lax.ppermute(values, axis, [(i, i ^ mask) for i in range(size)])  22.5 us
    pallas_call x4, Pallas kernels, weighted_call(): kernel_call(on_parts, 2 * tile_i * count * tile_k * rank, 2 * tile_i * co...  12.5 us
    pallas_call x2, Pallas kernels, slab_and_turn(): kernel_call(functools.partial(slab_kernel, first, chunk, steps), 2 * tile...  9.86 us
    pallas_call x1, Pallas kernels, local_products(): kernel_call(local_kernel, 2 * width * rank * (rank + rows), 2 * width * (...  2.4 us
  transfers between devices with their start and end apart: 31, of which 16 were waited for; matrix products, arithmetic and copies ran while one was open for 4% of the time, Pallas kernels for 28%

profile of v1, /device:TPU:0, one launch (start us, length us, event | category | flops | bytes accessed | tf_op | source)
XLA Modules:
  0.0 89.1 jit_solution(15691731542975833626)
XLA Ops:
  0.6 3.1 %collective-permute-start.21 = (bf16[128,256]{1,0:T(8,128)(2,1)}, bf16[128,256]{1,0:T(8,128)(2,1)S(1)}, u32[]{:S(2)}, u32[]{:S(2)}) collective-permute-start(bf16[128,256]{1,0:T(8,128)(2,1)} %refs_4_.3), channel_id=1, source_target_pairs={{0,1},{1,0},{2,3},{3,2},{4,5},{5,4},{6,7},{7,6},{8,9},{9,8},{10,11... | collective-permute-start | bytes 196616 | tf_op jit(solution)/shard_map/ppermute | solution.py:260
  3.8 2.4 %shard_map.85 = (f32[256,512]{1,0:T(8,128)S(1)}, f32[256,256]{1,0:T(8,128)S(1)}, f32[256,512]{1,0:T(8,128)S(1)}, bf16[128,256]{1,0:T(8,128)(2,1)S(1)}, bf16[128,256]{1,0:T(8,128)(2,1)S(1)}) custom-call(bf16[1024,256]{1,0:T(8,128)(2,1)} %column.1, bf16[128,256]{1,0:T(8,128)(2,1)} %second.1, bf16[128,256]{1,0:T(8,128)(2,1)} %refs_4_.3, bf16[512,1024]{1,0:T(8,128)(2,1)} %matrix.1), custom_call_target="tpu_custom_call" | custom-call | flops 402653184 | bytes 1572864 | tf_op jit(solution)/shard_map/pallas_call | solution.py:70
  6.3 1.6 %collective-permute-start = (f32[256,256]{1,0:T(8,128)S(1)}, f32[256,256]{1,0:T(8,128)S(1)}, u32[]{:S(2)}, u32[]{:S(2)}) collective-permute-start(f32[256,256]{1,0:T(8,128)S(1)} %constant_dynamic-slice_fusion.7), channel_id=1, source_target_pairs={{0,16},{16,0},{1,17},{17,1},{2,18},{18,2},{3,19},{19,3},{4,20},{20... | collective-permute-start | bytes 786440 | tf_op jit(solution)/shard_map/ppermute | solution.py:260
  7.9 4.9 %shard_map.86 = (f32[256,256]{1,0:T(8,128)S(1)}, bf16[64,128,256]{2,1,0:T(8,128)(2,1)}) custom-call(bf16[256,128,128]{2,1,0:T(8,128)(2,1)} %tensor.3, bf16[128,256]{1,0:T(8,128)(2,1)S(1)} %get-tuple-element.12.second, bf16[128,256]{1,0:T(8,128)(2,1)S(1)} %get-tuple-element.13.time), custom_call_target="tpu_custom_call" | custom-call | flops 1073741824 | bytes 8388608 | tf_op jit(solution)/shard_map/pallas_call | solution.py:144
  12.9 5.0 %shard_map.87 = (f32[256,256]{1,0:T(8,128)S(1)}, bf16[64,128,256]{2,1,0:T(8,128)(2,1)}) custom-call(bf16[256,128,128]{2,1,0:T(8,128)(2,1)} %tensor.3, bf16[128,256]{1,0:T(8,128)(2,1)S(1)} %get-tuple-element.12.second, bf16[128,256]{1,0:T(8,128)(2,1)S(1)} %get-tuple-element.13.time, f32[256,256]{1,0:T(8,128)S(1)} %get-tuple-element.14.refs_0_), custom_call_target="tpu_custom_call" | custom-call | flops 1073741824 | bytes 8388608 | tf_op jit(solution)/shard_map/pallas_call | solution.py:144
  18.0 1.6 %collective-permute-start.8 = (f32[64,512]{1,0:T(8,128)S(1)}, f32[64,512]{1,0:T(8,128)S(1)}, u32[]{:S(2)}, u32[]{:S(2)}) collective-permute-start(f32[64,512]{1,0:T(8,128)S(1)} %constant_dynamic-slice_fusion.2), channel_id=1, source_target_pairs={{0,8},{4,12},{8,0},{12,4},{1,9},{5,13},{9,1},{13,5},{2,10},{6,14},... | collective-permute-start | bytes 393224 | tf_op jit(solution)/shard_map/ppermute | solution.py:260
  21.9 2.5 %collective-permute-done.8 = f32[64,512]{1,0:T(8,128)S(1)} collective-permute-done((f32[64,512]{1,0:T(8,128)S(1)}, f32[64,512]{1,0:T(8,128)S(1)}, u32[]{:S(2)}, u32[]{:S(2)}) %collective-permute-start.8) | collective-permute-done | bytes 131104 | tf_op jit(solution)/shard_map/ppermute | solution.py:260
  24.5 2.7 %collective-permute-start.10 = (f32[64,512]{1,0:T(8,128)S(1)}, f32[64,512]{1,0:T(8,128)S(1)}, u32[]{:S(2)}, u32[]{:S(2)}) collective-permute-start(f32[64,512]{1,0:T(8,128)S(1)} %pad_maximum_fusion), channel_id=1, source_target_pairs={{0,2},{1,3},{2,0},{3,1},{4,6},{5,7},{6,4},{7,5},{8,10},{9,11},{10,... | collective-permute-start | bytes 393224 | tf_op jit(solution)/shard_map/ppermute | solution.py:260
  27.1 1.1 %collective-permute-start.11 = (f32[64,512]{1,0:T(8,128)S(1)}, f32[64,512]{1,0:T(8,128)S(1)}, u32[]{:S(2)}, u32[]{:S(2)}) collective-permute-start(f32[64,512]{1,0:T(8,128)S(1)} %pad_maximum_fusion), channel_id=1, source_target_pairs={{0,3},{1,2},{2,1},{3,0},{4,7},{5,6},{6,5},{7,4},{8,11},{9,10},{10,... | collective-permute-start | bytes 393224 | tf_op jit(solution)/shard_map/ppermute | solution.py:260
  28.9 2.7 %collective-permute-start.5 = (f32[64,256]{1,0:T(8,128)S(1)}, f32[64,256]{1,0:T(8,128)S(1)}, u32[]{:S(2)}, u32[]{:S(2)}) collective-permute-start(f32[64,256]{1,0:T(8,128)S(1)} %add_add_fusion.2), channel_id=1, source_target_pairs={{0,2},{1,3},{2,0},{3,1},{4,6},{5,7},{6,4},{7,5},{8,10},{9,11},{10,... | collective-permute-start | bytes 196616 | tf_op jit(solution)/shard_map/ppermute | solution.py:260
  31.6 5.1 %collective-permute-done.10 = f32[64,512]{1,0:T(8,128)S(1)} collective-permute-done((f32[64,512]{1,0:T(8,128)S(1)}, f32[64,512]{1,0:T(8,128)S(1)}, u32[]{:S(2)}, u32[]{:S(2)}) %collective-permute-start.10) | collective-permute-done | bytes 131104 | tf_op jit(solution)/shard_map/ppermute | solution.py:260
  36.8 2.6 %collective-permute-start.6 = (f32[64,256]{1,0:T(8,128)S(1)}, f32[64,256]{1,0:T(8,128)S(1)}, u32[]{:S(2)}, u32[]{:S(2)}) collective-permute-start(f32[64,256]{1,0:T(8,128)S(1)} %add_add_fusion.2), channel_id=1, source_target_pairs={{0,3},{1,2},{2,1},{3,0},{4,7},{5,6},{6,5},{7,4},{8,11},{9,10},{10,... | collective-permute-start | bytes 196616 | tf_op jit(solution)/shard_map/ppermute | solution.py:260
  39.4 2.1 %collective-permute-start.4 = (f32[64,256]{1,0:T(8,128)S(1)}, f32[64,256]{1,0:T(8,128)S(1)}, u32[]{:S(2)}, u32[]{:S(2)}) collective-permute-start(f32[64,256]{1,0:T(8,128)S(1)} %add_add_fusion.2), channel_id=1, source_target_pairs={{0,1},{1,0},{2,3},{3,2},{4,5},{5,4},{6,7},{7,6},{8,9},{9,8},{10,11... | collective-permute-start | bytes 196616 | tf_op jit(solution)/shard_map/ppermute | solution.py:260
  42.1 1.0 %collective-permute-done.6 = f32[64,256]{1,0:T(8,128)S(1)} collective-permute-done((f32[64,256]{1,0:T(8,128)S(1)}, f32[64,256]{1,0:T(8,128)S(1)}, u32[]{:S(2)}, u32[]{:S(2)}) %collective-permute-start.6) | collective-permute-done | bytes 65568 | tf_op jit(solution)/shard_map/ppermute | solution.py:260
  43.8 2.1 %collective-permute-done.12 = f32[64,256]{1,0:T(8,128)S(1)} collective-permute-done((f32[64,256]{1,0:T(8,128)S(1)}, f32[64,256]{1,0:T(8,128)S(1)}, u32[]{:S(2)}, u32[]{:S(2)}) %collective-permute-start.12) | collective-permute-done | bytes 65568 | tf_op jit(solution)/shard_map/ppermute | solution.py:260
  46.2 1.6 %collective-permute-start.13 = (bf16[64,256]{1,0:T(8,128)(2,1)S(1)}, bf16[64,256]{1,0:T(8,128)(2,1)S(1)}, u32[]{:S(2)}, u32[]{:S(2)}) collective-permute-start(bf16[64,256]{1,0:T(8,128)(2,1)S(1)} %fusion.17), channel_id=1, source_target_pairs={{0,8},{4,12},{8,0},{12,4},{1,9},{5,13},{9,1},{13,5},{2,10},{6,14},... | collective-permute-start | bytes 98312 | tf_op jit(solution)/shard_map/ppermute | solution.py:260
  47.8 1.2 %collective-permute-start.22 = (bf16[256,256]{1,0:T(8,128)(2,1)S(1)}, bf16[256,256]{1,0:T(8,128)(2,1)S(1)}, u32[]{:S(2)}, u32[]{:S(2)}) collective-permute-start(bf16[256,256]{1,0:T(8,128)(2,1)S(1)} %maximum_select_fusion.5), channel_id=1, source_target_pairs={{0,2},{1,3},{2,0},{3,1},{4,6},{5,7},{6,4},{7,5},{8,10},{9,11},{10,... | collective-permute-start | bytes 393224 | tf_op jit(solution)/shard_map/ppermute | solution.py:260
  50.2 2.2 %collective-permute-done.15 = bf16[64,256]{1,0:T(8,128)(2,1)S(1)} collective-permute-done((bf16[64,256]{1,0:T(8,128)(2,1)S(1)}, bf16[64,256]{1,0:T(8,128)(2,1)S(1)}, u32[]{:S(2)}, u32[]{:S(2)}) %collective-permute-start.15) | collective-permute-done | bytes 32800 | tf_op jit(solution)/shard_map/ppermute | solution.py:260
  53.2 3.1 %shard_map.89 = f32[64,256]{1,0:T(8,128)S(1)} custom-call(bf16[64,128,256]{2,1,0:T(8,128)(2,1)} %get-tuple-element.19.refs_0_, bf16[64,128,256]{2,1,0:T(8,128)(2,1)} %get-tuple-element.20.refs_1_, s32[1]{0:T(128)} %bitcast.3.refs_2_, bf16[256,256]{1,0:T(8,128)(2,1)S(1)} %maximum_select_fusion.4.refs_3_, bf16[128,256]{1,0:T(8,128)(2,1)S(1)} %copy-done.1), custom_call_target="tpu_custom_call" | custom-call | flops 1073741824 | bytes 4194304 | tf_op jit(solution)/shard_map/pallas_call | solution.py:229
  56.4 1.5 %collective-permute-start.16 = (f32[64,256]{1,0:T(8,128)S(1)}, f32[64,256]{1,0:T(8,128)S(1)}, u32[]{:S(2)}, u32[]{:S(2)}) collective-permute-start(f32[64,256]{1,0:T(8,128)S(1)} %shard_map.89), channel_id=1, source_target_pairs={{0,16},{16,0},{1,17},{17,1},{2,18},{18,2},{3,19},{19,3},{4,20},{20... | collective-permute-start | bytes 196616 | tf_op jit(solution)/shard_map/ppermute | solution.py:260
  57.9 3.2 %shard_map.88 = f32[64,256]{1,0:T(8,128)S(1)} custom-call(bf16[64,128,256]{2,1,0:T(8,128)(2,1)} %get-tuple-element.19.refs_0_, bf16[64,128,256]{2,1,0:T(8,128)(2,1)} %get-tuple-element.20.refs_1_, s32[1]{0:T(128)} %bitcast.2.refs_2_, bf16[256,256]{1,0:T(8,128)(2,1)S(1)} %maximum_select_fusion.4.refs_3_, bf16[128,256]{1,0:T(8,128)(2,1)S(1)} %copy-done.1), custom_call_target="tpu_custom_call" | custom-call | flops 1073741824 | bytes 4194304 | tf_op jit(solution)/shard_map/pallas_call | solution.py:229
  61.1 1.8 %collective-permute-start.18 = (f32[64,256]{1,0:T(8,128)S(1)}, f32[64,256]{1,0:T(8,128)S(1)}, u32[]{:S(2)}, u32[]{:S(2)}) collective-permute-start(f32[64,256]{1,0:T(8,128)S(1)} %add.173), channel_id=1, source_target_pairs={{0,2},{1,3},{2,0},{3,1},{4,6},{5,7},{6,4},{7,5},{8,10},{9,11},{10,... | collective-permute-start | bytes 196616 | tf_op jit(solution)/shard_map/ppermute | solution.py:260
  63.0 2.6 %collective-permute-start.19 = (f32[64,256]{1,0:T(8,128)S(1)}, f32[64,256]{1,0:T(8,128)S(1)}, u32[]{:S(2)}, u32[]{:S(2)}) collective-permute-start(f32[64,256]{1,0:T(8,128)S(1)} %add.173), channel_id=1, source_target_pairs={{0,3},{1,2},{2,1},{3,0},{4,7},{5,6},{6,5},{7,4},{8,11},{9,10},{10,... | collective-permute-start | bytes 196616 | tf_op jit(solution)/shard_map/ppermute | solution.py:260
  66.9 2.1 %collective-permute-done.19 = f32[64,256]{1,0:T(8,128)S(1)} collective-permute-done((f32[64,256]{1,0:T(8,128)S(1)}, f32[64,256]{1,0:T(8,128)S(1)}, u32[]{:S(2)}, u32[]{:S(2)}) %collective-permute-start.19) | collective-permute-done | bytes 65568 | tf_op jit(solution)/shard_map/ppermute | solution.py:260
  69.9 1.1 %collective-permute-start.23 = (bf16[64,256]{1,0:T(8,128)(2,1)S(1)}, bf16[64,256]{1,0:T(8,128)(2,1)S(1)}, u32[]{:S(2)}, u32[]{:S(2)}) collective-permute-start(bf16[64,256]{1,0:T(8,128)(2,1)S(1)} %divide_convert_fusion.1.refs_4_), channel_id=1, source_target_pairs={{0,16},{16,0},{1,17},{17,1},{2,18},{18,2},{3,19},{19,3},{4,20},{20... | collective-permute-start | bytes 98312 | tf_op jit(solution)/shard_map/ppermute | solution.py:260
  71.0 3.1 %shard_map.90.refs_5_ = f32[128,256]{1,0:T(8,128)S(1)} custom-call(bf16[64,128,256]{2,1,0:T(8,128)(2,1)} %get-tuple-element.19.refs_0_, bf16[64,128,256]{2,1,0:T(8,128)(2,1)} %get-tuple-element.20.refs_1_, s32[1]{0:T(128)} %bitcast.2.refs_2_, bf16[256,256]{1,0:T(8,128)(2,1)S(1)} %maximum_select_fusion.4.refs_3_, bf16[64,256]{1,0:T(8,128)(2,1)S(1)} %divide_convert_fusion.1.refs_4_), custom_call_target="tpu_custom_call" | custom-call | flops 1073741824 | bytes 4194304 | tf_op jit(solution)/shard_map/pallas_call | solution.py:229
  74.2 1.0 %collective-permute-start.28 = (bf16[128,256]{1,0:T(8,128)(2,1)S(1)}, bf16[128,256]{1,0:T(8,128)(2,1)S(1)}, u32[]{:S(2)}, u32[]{:S(2)}) collective-permute-start(bf16[128,256]{1,0:T(8,128)(2,1)S(1)} %maximum_select_fusion.9), channel_id=1, source_target_pairs={{0,8},{4,12},{8,0},{12,4},{1,9},{5,13},{9,1},{13,5},{2,10},{6,14},... | collective-permute-start | bytes 196616 | tf_op jit(solution)/shard_map/ppermute | solution.py:260
  75.1 3.1 %shard_map.91 = f32[128,256]{1,0:T(8,128)S(1)} custom-call(bf16[64,128,256]{2,1,0:T(8,128)(2,1)} %get-tuple-element.19.refs_0_, bf16[64,128,256]{2,1,0:T(8,128)(2,1)} %get-tuple-element.20.refs_1_, s32[1]{0:T(128)} %bitcast.3.refs_2_, bf16[256,256]{1,0:T(8,128)(2,1)S(1)} %maximum_select_fusion.4.refs_3_, ...), custom_call_target="tpu_custom_call" | custom-call | flops 1073741824 | bytes 4194304 | tf_op jit(solution)/shard_map/pallas_call | solution.py:229
  79.6 1.3 %collective-permute-start.26 = (f32[64,256]{1,0:T(8,128)S(1)}, f32[64,256]{1,0:T(8,128)S(1)}, u32[]{:S(2)}, u32[]{:S(2)}) collective-permute-start(f32[64,256]{1,0:T(8,128)S(1)} %dynamic-slice_add_fusion.2), channel_id=1, source_target_pairs={{0,16},{4,20},{8,24},{12,28},{16,0},{20,4},{24,8},{28,12},{1,17},{... | collective-permute-start | bytes 196616 | tf_op jit(solution)/shard_map/ppermute | solution.py:260
  80.9 1.4 %collective-permute-start.27 = (f32[64,256]{1,0:T(8,128)S(1)}, f32[64,256]{1,0:T(8,128)S(1)}, u32[]{:S(2)}, u32[]{:S(2)}) collective-permute-start(f32[64,256]{1,0:T(8,128)S(1)} %dynamic-slice_add_fusion.2), channel_id=1, source_target_pairs={{0,24},{4,28},{8,16},{12,20},{16,8},{20,12},{24,0},{28,4},{1,25},{... | collective-permute-start | bytes 196616 | tf_op jit(solution)/shard_map/ppermute | solution.py:260
  84.2 1.8 %collective-permute-done.27 = f32[64,256]{1,0:T(8,128)S(1)} collective-permute-done((f32[64,256]{1,0:T(8,128)S(1)}, f32[64,256]{1,0:T(8,128)S(1)}, u32[]{:S(2)}, u32[]{:S(2)}) %collective-permute-start.27) | collective-permute-done | bytes 65568 | tf_op jit(solution)/shard_map/ppermute | solution.py:260
  86.0 1.1 %collective-permute-done.25 = f32[64,256]{1,0:T(8,128)S(1)} collective-permute-done((f32[64,256]{1,0:T(8,128)S(1)}, f32[64,256]{1,0:T(8,128)S(1)}, u32[]{:S(2)}, u32[]{:S(2)}) %collective-permute-start.25) | collective-permute-done | bytes 65568 | tf_op jit(solution)/shard_map/ppermute | solution.py:260
  (80 shorter events, 14.2 us)
Async XLA Ops:
  0.6 41.2 %copy-start = (bf16[256,256]{1,0:T(8,128)(2,1)S(1)}, bf16[256,256]{1,0:T(8,128)(2,1)}, u32[]{:S(2)}) copy-start(bf16[256,256]{1,0:T(8,128)(2,1)} %param.8) | copy-start | bytes 393220
  0.6 47.1 %collective-permute-start.21 = (bf16[128,256]{1,0:T(8,128)(2,1)}, bf16[128,256]{1,0:T(8,128)(2,1)S(1)}, u32[]{:S(2)}, u32[]{:S(2)}) collective-permute-start(bf16[128,256]{1,0:T(8,128)(2,1)} %refs_4_.3), channel_id=1, source_target_pairs={{0,1},{1,0},{2,3},{3,2},{4,5},{5,4},{6,7},{7,6},{8,9},{9,8},{10,11... | collective-permute-start | bytes 196616 | tf_op jit(solution)/shard_map/ppermute | solution.py:260
  6.2 11.7 %collective-permute-start.7 = (f32[128,512]{1,0:T(8,128)S(1)}, f32[128,512]{1,0:T(8,128)S(1)}, u32[]{:S(2)}, u32[]{:S(2)}) collective-permute-start(f32[128,512]{1,0:T(8,128)S(1)} %constant_dynamic-slice_fusion.3), channel_id=1, source_target_pairs={{0,4},{4,0},{8,12},{12,8},{1,5},{5,1},{9,13},{13,9},{2,6},{6,2},{1... | collective-permute-start | bytes 786440 | tf_op jit(solution)/shard_map/ppermute | solution.py:260
  6.3 13.3 %collective-permute-start = (f32[256,256]{1,0:T(8,128)S(1)}, f32[256,256]{1,0:T(8,128)S(1)}, u32[]{:S(2)}, u32[]{:S(2)}) collective-permute-start(f32[256,256]{1,0:T(8,128)S(1)} %constant_dynamic-slice_fusion.7), channel_id=1, source_target_pairs={{0,16},{16,0},{1,17},{17,1},{2,18},{18,2},{3,19},{19,3},{4,20},{20... | collective-permute-start | bytes 786440 | tf_op jit(solution)/shard_map/ppermute | solution.py:260
  18.0 6.4 %collective-permute-start.8 = (f32[64,512]{1,0:T(8,128)S(1)}, f32[64,512]{1,0:T(8,128)S(1)}, u32[]{:S(2)}, u32[]{:S(2)}) collective-permute-start(f32[64,512]{1,0:T(8,128)S(1)} %constant_dynamic-slice_fusion.2), channel_id=1, source_target_pairs={{0,8},{4,12},{8,0},{12,4},{1,9},{5,13},{9,1},{13,5},{2,10},{6,14},... | collective-permute-start | bytes 393224 | tf_op jit(solution)/shard_map/ppermute | solution.py:260
  19.7 7.5 %collective-permute-start.2 = (f32[64,256]{1,0:T(8,128)S(1)}, f32[64,256]{1,0:T(8,128)S(1)}, u32[]{:S(2)}, u32[]{:S(2)}) collective-permute-start(f32[64,256]{1,0:T(8,128)S(1)} %get-tuple-element.26), channel_id=1, source_target_pairs={{0,8},{4,12},{8,0},{12,4},{1,9},{5,13},{9,1},{13,5},{2,10},{6,14},... | collective-permute-start | bytes 196616 | tf_op jit(solution)/shard_map/ppermute | solution.py:260
  20.2 8.0 %collective-permute-start.3 = (f32[64,256]{1,0:T(8,128)S(1)}, f32[64,256]{1,0:T(8,128)S(1)}, u32[]{:S(2)}, u32[]{:S(2)}) collective-permute-start(f32[64,256]{1,0:T(8,128)S(1)} %get-tuple-element.25), channel_id=1, source_target_pairs={{0,12},{4,8},{8,4},{12,0},{1,13},{5,9},{9,5},{13,1},{2,14},{6,10},... | collective-permute-start | bytes 196616 | tf_op jit(solution)/shard_map/ppermute | solution.py:260
  21.0 7.9 %collective-permute-start.1 = (f32[64,256]{1,0:T(8,128)S(1)}, f32[64,256]{1,0:T(8,128)S(1)}, u32[]{:S(2)}, u32[]{:S(2)}) collective-permute-start(f32[64,256]{1,0:T(8,128)S(1)} %get-tuple-element.24), channel_id=1, source_target_pairs={{0,4},{4,0},{8,12},{12,8},{1,5},{5,1},{9,13},{13,9},{2,6},{6,2},{1... | collective-permute-start | bytes 196616 | tf_op jit(solution)/shard_map/ppermute | solution.py:260
  24.5 12.3 %collective-permute-start.10 = (f32[64,512]{1,0:T(8,128)S(1)}, f32[64,512]{1,0:T(8,128)S(1)}, u32[]{:S(2)}, u32[]{:S(2)}) collective-permute-start(f32[64,512]{1,0:T(8,128)S(1)} %pad_maximum_fusion), channel_id=1, source_target_pairs={{0,2},{1,3},{2,0},{3,1},{4,6},{5,7},{6,4},{7,5},{8,10},{9,11},{10,... | collective-permute-start | bytes 393224 | tf_op jit(solution)/shard_map/ppermute | solution.py:260
  27.1 12.3 %collective-permute-start.11 = (f32[64,512]{1,0:T(8,128)S(1)}, f32[64,512]{1,0:T(8,128)S(1)}, u32[]{:S(2)}, u32[]{:S(2)}) collective-permute-start(f32[64,512]{1,0:T(8,128)S(1)} %pad_maximum_fusion), channel_id=1, source_target_pairs={{0,3},{1,2},{2,1},{3,0},{4,7},{5,6},{6,5},{7,4},{8,11},{9,10},{10,... | collective-permute-start | bytes 393224 | tf_op jit(solution)/shard_map/ppermute | solution.py:260
  28.2 13.3 %collective-permute-start.9 = (f32[64,512]{1,0:T(8,128)S(1)}, f32[64,512]{1,0:T(8,128)S(1)}, u32[]{:S(2)}, u32[]{:S(2)}) collective-permute-start(f32[64,512]{1,0:T(8,128)S(1)} %pad_maximum_fusion), channel_id=1, source_target_pairs={{0,1},{1,0},{2,3},{3,2},{4,5},{5,4},{6,7},{7,6},{8,9},{9,8},{10,11... | collective-permute-start | bytes 393224 | tf_op jit(solution)/shard_map/ppermute | solution.py:260
  28.9 13.1 %collective-permute-start.5 = (f32[64,256]{1,0:T(8,128)S(1)}, f32[64,256]{1,0:T(8,128)S(1)}, u32[]{:S(2)}, u32[]{:S(2)}) collective-permute-start(f32[64,256]{1,0:T(8,128)S(1)} %add_add_fusion.2), channel_id=1, source_target_pairs={{0,2},{1,3},{2,0},{3,1},{4,6},{5,7},{6,4},{7,5},{8,10},{9,11},{10,... | collective-permute-start | bytes 196616 | tf_op jit(solution)/shard_map/ppermute | solution.py:260
  36.8 6.3 %collective-permute-start.6 = (f32[64,256]{1,0:T(8,128)S(1)}, f32[64,256]{1,0:T(8,128)S(1)}, u32[]{:S(2)}, u32[]{:S(2)}) collective-permute-start(f32[64,256]{1,0:T(8,128)S(1)} %add_add_fusion.2), channel_id=1, source_target_pairs={{0,3},{1,2},{2,1},{3,0},{4,7},{5,6},{6,5},{7,4},{8,11},{9,10},{10,... | collective-permute-start | bytes 196616 | tf_op jit(solution)/shard_map/ppermute | solution.py:260
  39.4 4.4 %collective-permute-start.4 = (f32[64,256]{1,0:T(8,128)S(1)}, f32[64,256]{1,0:T(8,128)S(1)}, u32[]{:S(2)}, u32[]{:S(2)}) collective-permute-start(f32[64,256]{1,0:T(8,128)S(1)} %add_add_fusion.2), channel_id=1, source_target_pairs={{0,1},{1,0},{2,3},{3,2},{4,5},{5,4},{6,7},{7,6},{8,9},{9,8},{10,11... | collective-permute-start | bytes 196616 | tf_op jit(solution)/shard_map/ppermute | solution.py:260
  41.6 4.3 %collective-permute-start.12 = (f32[64,256]{1,0:T(8,128)S(1)}, f32[64,256]{1,0:T(8,128)S(1)}, u32[]{:S(2)}, u32[]{:S(2)}) collective-permute-start(f32[64,256]{1,0:T(8,128)S(1)} %slice.19), channel_id=1, source_target_pairs={{0,16},{16,0},{1,17},{17,1},{2,18},{18,2},{3,19},{19,3},{4,20},{20... | collective-permute-start | bytes 196616 | tf_op jit(solution)/shard_map/ppermute | solution.py:260
  46.2 4.0 %collective-permute-start.13 = (bf16[64,256]{1,0:T(8,128)(2,1)S(1)}, bf16[64,256]{1,0:T(8,128)(2,1)S(1)}, u32[]{:S(2)}, u32[]{:S(2)}) collective-permute-start(bf16[64,256]{1,0:T(8,128)(2,1)S(1)} %fusion.17), channel_id=1, source_target_pairs={{0,8},{4,12},{8,0},{12,4},{1,9},{5,13},{9,1},{13,5},{2,10},{6,14},... | collective-permute-start | bytes 98312 | tf_op jit(solution)/shard_map/ppermute | solution.py:260
  47.8 18.0 %collective-permute-start.22 = (bf16[256,256]{1,0:T(8,128)(2,1)S(1)}, bf16[256,256]{1,0:T(8,128)(2,1)S(1)}, u32[]{:S(2)}, u32[]{:S(2)}) collective-permute-start(bf16[256,256]{1,0:T(8,128)(2,1)S(1)} %maximum_select_fusion.5), channel_id=1, source_target_pairs={{0,2},{1,3},{2,0},{3,1},{4,6},{5,7},{6,4},{7,5},{8,10},{9,11},{10,... | collective-permute-start | bytes 393224 | tf_op jit(solution)/shard_map/ppermute | solution.py:260
  49.0 3.3 %collective-permute-start.15 = (bf16[64,256]{1,0:T(8,128)(2,1)S(1)}, bf16[64,256]{1,0:T(8,128)(2,1)S(1)}, u32[]{:S(2)}, u32[]{:S(2)}) collective-permute-start(bf16[64,256]{1,0:T(8,128)(2,1)S(1)} %fusion.17), channel_id=1, source_target_pairs={{0,12},{4,8},{8,4},{12,0},{1,13},{5,9},{9,5},{13,1},{2,14},{6,10},... | collective-permute-start | bytes 98312 | tf_op jit(solution)/shard_map/ppermute | solution.py:260
  49.0 3.3 %collective-permute-start.14 = (bf16[64,256]{1,0:T(8,128)(2,1)S(1)}, bf16[64,256]{1,0:T(8,128)(2,1)S(1)}, u32[]{:S(2)}, u32[]{:S(2)}) collective-permute-start(bf16[64,256]{1,0:T(8,128)(2,1)S(1)} %fusion.17), channel_id=1, source_target_pairs={{0,4},{4,0},{8,12},{12,8},{1,5},{5,1},{9,13},{13,9},{2,6},{6,2},{1... | collective-permute-start | bytes 98312 | tf_op jit(solution)/shard_map/ppermute | solution.py:260
  52.7 12.9 %collective-permute-start.20 = (bf16[256,256]{1,0:T(8,128)(2,1)S(1)}, bf16[256,256]{1,0:T(8,128)(2,1)S(1)}, u32[]{:S(2)}, u32[]{:S(2)}) collective-permute-start(bf16[256,256]{1,0:T(8,128)(2,1)S(1)} %maximum_select_fusion.4.refs_3_), channel_id=1, source_target_pairs={{0,16},{16,0},{1,17},{17,1},{2,18},{18,2},{3,19},{19,3},{4,20},{20... | collective-permute-start | bytes 393224 | tf_op jit(solution)/shard_map/ppermute | solution.py:260
  56.4 4.7 %collective-permute-start.16 = (f32[64,256]{1,0:T(8,128)S(1)}, f32[64,256]{1,0:T(8,128)S(1)}, u32[]{:S(2)}, u32[]{:S(2)}) collective-permute-start(f32[64,256]{1,0:T(8,128)S(1)} %shard_map.89), channel_id=1, source_target_pairs={{0,16},{16,0},{1,17},{17,1},{2,18},{18,2},{3,19},{19,3},{4,20},{20... | collective-permute-start | bytes 196616 | tf_op jit(solution)/shard_map/ppermute | solution.py:260
  61.1 5.8 %collective-permute-start.18 = (f32[64,256]{1,0:T(8,128)S(1)}, f32[64,256]{1,0:T(8,128)S(1)}, u32[]{:S(2)}, u32[]{:S(2)}) collective-permute-start(f32[64,256]{1,0:T(8,128)S(1)} %add.173), channel_id=1, source_target_pairs={{0,2},{1,3},{2,0},{3,1},{4,6},{5,7},{6,4},{7,5},{8,10},{9,11},{10,... | collective-permute-start | bytes 196616 | tf_op jit(solution)/shard_map/ppermute | solution.py:260
  63.0 6.1 %collective-permute-start.19 = (f32[64,256]{1,0:T(8,128)S(1)}, f32[64,256]{1,0:T(8,128)S(1)}, u32[]{:S(2)}, u32[]{:S(2)}) collective-permute-start(f32[64,256]{1,0:T(8,128)S(1)} %add.173), channel_id=1, source_target_pairs={{0,3},{1,2},{2,1},{3,0},{4,7},{5,6},{6,5},{7,4},{8,11},{9,10},{10,... | collective-permute-start | bytes 196616 | tf_op jit(solution)/shard_map/ppermute | solution.py:260
  65.6 4.3 %collective-permute-start.17 = (f32[64,256]{1,0:T(8,128)S(1)}, f32[64,256]{1,0:T(8,128)S(1)}, u32[]{:S(2)}, u32[]{:S(2)}) collective-permute-start(f32[64,256]{1,0:T(8,128)S(1)} %add.173), channel_id=1, source_target_pairs={{0,1},{1,0},{2,3},{3,2},{4,5},{5,4},{6,7},{7,6},{8,9},{9,8},{10,11... | collective-permute-start | bytes 196616 | tf_op jit(solution)/shard_map/ppermute | solution.py:260
  69.9 4.2 %collective-permute-start.23 = (bf16[64,256]{1,0:T(8,128)(2,1)S(1)}, bf16[64,256]{1,0:T(8,128)(2,1)S(1)}, u32[]{:S(2)}, u32[]{:S(2)}) collective-permute-start(bf16[64,256]{1,0:T(8,128)(2,1)S(1)} %divide_convert_fusion.1.refs_4_), channel_id=1, source_target_pairs={{0,16},{16,0},{1,17},{17,1},{2,18},{18,2},{3,19},{19,3},{4,20},{20... | collective-permute-start | bytes 98312 | tf_op jit(solution)/shard_map/ppermute | solution.py:260
  74.2 4.3 %collective-permute-start.28 = (bf16[128,256]{1,0:T(8,128)(2,1)S(1)}, bf16[128,256]{1,0:T(8,128)(2,1)S(1)}, u32[]{:S(2)}, u32[]{:S(2)}) collective-permute-start(bf16[128,256]{1,0:T(8,128)(2,1)S(1)} %maximum_select_fusion.9), channel_id=1, source_target_pairs={{0,8},{4,12},{8,0},{12,4},{1,9},{5,13},{9,1},{13,5},{2,10},{6,14},... | collective-permute-start | bytes 196616 | tf_op jit(solution)/shard_map/ppermute | solution.py:260
  78.2 1.3 %collective-permute-start.24 = (f32[64,256]{1,0:T(8,128)S(1)}, f32[64,256]{1,0:T(8,128)S(1)}, u32[]{:S(2)}, u32[]{:S(2)}) collective-permute-start(f32[64,256]{1,0:T(8,128)S(1)} %constant_dynamic-slice_fusion), channel_id=1, source_target_pairs={{0,4},{4,0},{8,12},{12,8},{1,5},{5,1},{9,13},{13,9},{2,6},{6,2},{1... | collective-permute-start | bytes 196616 | tf_op jit(solution)/shard_map/ppermute | solution.py:260
  78.5 4.6 %collective-permute-start.29 = (bf16[256,256]{1,0:T(8,128)(2,1)S(1)}, bf16[256,256]{1,0:T(8,128)(2,1)S(1)}, u32[]{:S(2)}, u32[]{:S(2)}) collective-permute-start(bf16[256,256]{1,0:T(8,128)(2,1)S(1)} %maximum_select_fusion.6), channel_id=1, source_target_pairs={{0,4},{4,0},{8,12},{12,8},{1,5},{5,1},{9,13},{13,9},{2,6},{6,2},{1... | collective-permute-start | bytes 393224 | tf_op jit(solution)/shard_map/ppermute | solution.py:260
  79.6 4.6 %collective-permute-start.26 = (f32[64,256]{1,0:T(8,128)S(1)}, f32[64,256]{1,0:T(8,128)S(1)}, u32[]{:S(2)}, u32[]{:S(2)}) collective-permute-start(f32[64,256]{1,0:T(8,128)S(1)} %dynamic-slice_add_fusion.2), channel_id=1, source_target_pairs={{0,16},{4,20},{8,24},{12,28},{16,0},{20,4},{24,8},{28,12},{1,17},{... | collective-permute-start | bytes 196616 | tf_op jit(solution)/shard_map/ppermute | solution.py:260
  80.9 5.2 %collective-permute-start.27 = (f32[64,256]{1,0:T(8,128)S(1)}, f32[64,256]{1,0:T(8,128)S(1)}, u32[]{:S(2)}, u32[]{:S(2)}) collective-permute-start(f32[64,256]{1,0:T(8,128)S(1)} %dynamic-slice_add_fusion.2), channel_id=1, source_target_pairs={{0,24},{4,28},{8,16},{12,20},{16,8},{20,12},{24,0},{28,4},{1,25},{... | collective-permute-start | bytes 196616 | tf_op jit(solution)/shard_map/ppermute | solution.py:260
  82.2 4.9 %collective-permute-start.25 = (f32[64,256]{1,0:T(8,128)S(1)}, f32[64,256]{1,0:T(8,128)S(1)}, u32[]{:S(2)}, u32[]{:S(2)}) collective-permute-start(f32[64,256]{1,0:T(8,128)S(1)} %dynamic-slice_add_fusion.2), channel_id=1, source_target_pairs={{0,8},{4,12},{8,0},{12,4},{16,24},{20,28},{24,16},{28,20},{1,9},{5... | collective-permute-start | bytes 196616 | tf_op jit(solution)/shard_map/ppermute | solution.py:260
  87.2 1.3 %collective-permute-start.30 = (bf16[64,256]{1,0:T(8,128)(2,1)S(1)}, bf16[64,256]{1,0:T(8,128)(2,1)S(1)}, u32[]{:S(2)}, u32[]{:S(2)}) collective-permute-start(bf16[64,256]{1,0:T(8,128)(2,1)S(1)} %divide_convert_fusion), channel_id=1, source_target_pairs={{0,4},{4,0},{8,12},{12,8},{1,5},{5,1},{9,13},{13,9},{2,6},{6,2},{1... | collective-permute-start | bytes 98312 | tf_op jit(solution)/shard_map/ppermute | solution.py:260
  (3 other events, 42.5 us)
